TPU v7x, 32 devices: a whole 2x2x4 slice. The times are simulated.
32 devices in a mesh: parts: 2 (over x), leaf: 16 (over z, y, core).
Axes of the slice: x: 2, y: 2, z: 4, core: 2. Of those that a mesh axis runs over, the one named last changes fastest.
Arguments:
- right_sides: bfloat16 [128, 16384], P('parts', 'leaf'), parts along dimension 0, may hold values from -6 to 6
- near_list: int32 [32, 3], P(('parts', 'leaf')), parts along dimension 0, may hold values from 0 to 15, as said below
- near_blocks: bfloat16 [32, 3, 1024, 1024], P(('parts', 'leaf')), parts along dimension 0, may hold values from -0.02734375 to 0.02734375
- inverse_list: int32 [32, 2], P(('parts', 'leaf')), parts along dimension 0, may hold values from 0 to 15, as said below
- inverse_blocks: bfloat16 [32, 2, 1024, 1024], P(('parts', 'leaf')), parts along dimension 0, may hold values from -0.03125 to 0.03125
- leaf_bases: bfloat16 [32, 1024, 128], P(('parts', 'leaf')), parts along dimension 0, may hold values from -0.1875 to 0.1875
- transfers: bfloat16 [2, 2, 128, 128], replicated, may hold values from -0.375 to 0.375
- couple_list: int32 [32, 3, 4], P(('parts', 'leaf')), parts along dimension 0, may hold values from 0 to 15, as said below
- couple_blocks: bfloat16 [32, 3, 4, 128, 128], P(('parts', 'leaf')), parts along dimension 0, may hold values from -0.125 to 0.125
Outputs:
- solution: float32 [128, 16384], P('parts', 'leaf'), parts along dimension 0
- residual: float32 [128, 16384], P('parts', 'leaf'), parts along dimension 0
There are 2 independent parts, one for each index of `parts`. A program takes and returns all parts, laid end to end along the dimension named above; an argument that names none is the same for every part. Nothing has to cross between parts.
Inputs may be any that keep to these rules, and one draw needn't show every extreme that they name: `near_list`: entry [i, s] lies within 2 of i. `inverse_list`: entry [i, s] lies within 2 of i. `couple_list`: entry [i, l, k] names a cluster of level l, below 16 // 2 ** l.
All inputs are finite; a program needn't handle non-finite values.
Results may differ from a plain program's by a relative error of at most 0.014.
Values may be sent and summed in bfloat16 or wider, within the bound.
A program may use at most 64 MiB of HBM per device.

v0:
```python
import jax
import jax.numpy as jnp
from jax import lax
from jax.sharding import PartitionSpec as P

REACH = 2


exact_mode = lax.Precision.HIGHEST


def from_behind(value, axis, steps):
    count = lax.axis_size(axis)
    first, last = (max(0, -steps), min(count, count - steps))
    return lax.ppermute(value, axis, [(source, source + steps) for source in range(first, last)])


def partner(value, axis, apart):
    mask = 2**apart
    pairs = [(source, source ^ mask) for source in range(lax.axis_size(axis))]
    return lax.ppermute(value, axis, pairs)


def neighbourhood(half_vector):
    received = {0: half_vector}
    for offset in range(-REACH, REACH + 1):
        if offset != 0:
            received[offset] = from_behind(half_vector, "leaf", -offset)
    return jnp.stack([received[offset] for offset in range(-REACH, REACH + 1)])


def apply_slots(window, relative, blocks):
    running = jnp.zeros(window.shape[1:], jnp.float32)
    for slot_index in range(blocks.shape[0]):
        chosen = lax.dynamic_index_in_dim(window, relative[slot_index], 0, keepdims=False)
        running = running + jnp.dot(chosen, blocks[slot_index], preferred_element_type=jnp.float32)
    return running


def select_map(child_maps, position):
    return lax.dynamic_index_in_dim(child_maps, position, 0, keepdims=False)


def lift_all(coeffs, child_maps):
    grouped = coeffs.reshape(coeffs.shape[0] // 2, 2, coeffs.shape[1], coeffs.shape[2])
    left_part = jnp.einsum(
        "prs,st->prt", grouped[:, 0], child_maps[0], preferred_element_type=jnp.float32
    )
    right_part = jnp.einsum(
        "prs,st->prt", grouped[:, 1], child_maps[1], preferred_element_type=jnp.float32
    )
    return (left_part + right_part).astype(jnp.bfloat16)


def far_term(half_vector, leaf_bases, transfers, couple_list, couple_blocks, first_bit, second_bit):
    coeff_zero = jnp.dot(half_vector, leaf_bases[0], preferred_element_type=jnp.float32).astype(
        jnp.bfloat16
    )
    table_zero = lax.all_gather(coeff_zero[None], "leaf", axis=0, tiled=True)
    table_one = lift_all(table_zero, transfers[0])
    table_two = lift_all(table_one, transfers[1])
    fields = []
    for tree_level, coeff_table in enumerate((table_zero, table_one, table_two)):
        chosen = jnp.take(coeff_table, couple_list[0, tree_level], axis=0)
        fields.append(
            jnp.einsum(
                "krs,kst->rt",
                chosen,
                couple_blocks[0, tree_level],
                preferred_element_type=jnp.float32,
            )
        )
    upper_fields = jnp.stack((fields[1], fields[2]))
    paired = upper_fields + partner(upper_fields, "leaf", 0)
    quad_sum = paired[1] + partner(paired[1], "leaf", 1)
    upper_map = select_map(transfers[1], second_bit).astype(jnp.float32)
    down_one = paired[0] + jnp.dot(quad_sum, upper_map.T, precision=exact_mode)
    lower_map = select_map(transfers[0], first_bit).astype(jnp.float32)
    leaf_field = fields[0] + jnp.dot(down_one, lower_map.T, precision=exact_mode)
    return jnp.einsum(
        "rs,js->rj",
        leaf_field.astype(jnp.bfloat16),
        leaf_bases[0],
        preferred_element_type=jnp.float32,
    )


def shards(
    right_sides,
    near_list,
    near_blocks,
    inverse_list,
    inverse_blocks,
    leaf_bases,
    transfers,
    couple_list,
    couple_blocks,
):
    device_index = lax.axis_index("leaf")
    first_bit = device_index % 2
    second_bit = device_index // 2 % 2
    near_relative = near_list[0] - device_index + REACH
    inverse_relative = inverse_list[0] - device_index + REACH

    def operate(half_vector):
        near_part = apply_slots(neighbourhood(half_vector), near_relative, near_blocks[0])
        far_part = far_term(
            half_vector, leaf_bases, transfers, couple_list, couple_blocks, first_bit, second_bit
        )
        return half_vector.astype(jnp.float32) + near_part + far_part

    def precondition(half_vector):
        return half_vector.astype(jnp.float32) + apply_slots(
            neighbourhood(half_vector), inverse_relative, inverse_blocks[0]
        )

    wide_sides = right_sides.astype(jnp.float32)
    iterate_one = precondition(right_sides)
    residual_one = wide_sides - operate(iterate_one.astype(jnp.bfloat16))
    solution = iterate_one + precondition(residual_one.astype(jnp.bfloat16))
    residual = wide_sides - operate(solution.astype(jnp.bfloat16))
    return (solution, residual)


def solution(mesh):
    return jax.shard_map(
        shards,
        mesh=mesh,
        in_specs=(
            P("parts", "leaf"),
            P(("parts", "leaf"), None),
            P(("parts", "leaf"), None, None, None),
            P(("parts", "leaf"), None),
            P(("parts", "leaf"), None, None, None),
            P(("parts", "leaf"), None, None),
            P(),
            P(("parts", "leaf"), None, None),
            P(("parts", "leaf"), None, None, None, None),
        ),
        out_specs=(P("parts", "leaf"), P("parts", "leaf")),
        check_vma=False,
    )
```

profile of v0, /device:TPU:0, one launch (start us, length us, event | category | flops | bytes accessed | tf_op | source)
XLA Modules:
  0.0 142.7 jit_solution(14897940003670410448)
XLA Ops:
  0.7 5.0 %collective-permute-start = (bf16[64,1024]{1,0:T(8,128)(2,1)}, bf16[64,1024]{1,0:T(8,128)(2,1)S(1)}, u32[]{:S(2)}, u32[]{:S(2)}) collective-permute-start(bf16[64,1024]{1,0:T(8,128)(2,1)} %param.15), channel_id=1, source_target_pairs={{0,2},{1,3},{2,4},{3,5},{4,6},{5,7},{6,8},{7,9},{8,10},{9,11},{10,... | collective-permute-start | bytes 393224 | tf_op jit(solution)/shard_map/ppermute | solution.py:15
  5.7 1.5 %collective-permute-start.1 = (bf16[64,1024]{1,0:T(8,128)(2,1)}, bf16[64,1024]{1,0:T(8,128)(2,1)S(1)}, u32[]{:S(2)}, u32[]{:S(2)}) collective-permute-start(bf16[64,1024]{1,0:T(8,128)(2,1)} %param.15), channel_id=1, source_target_pairs={{0,1},{1,2},{2,3},{3,4},{4,5},{5,6},{6,7},{7,8},{8,9},{9,10},{10,1... | collective-permute-start | bytes 393224 | tf_op jit(solution)/shard_map/ppermute | solution.py:15
  7.2 1.3 collective-permute-start.2
  8.5 1.3 collective-permute-start.3
  9.8 0.7 subtract_add_fusion.1
  10.5 0.6 fusion.200
  11.0 0.7 compare_and_fusion.1
  11.7 0.9 fusion.198
  12.6 0.7 subtract_add_fusion
  13.3 0.7 fusion.199
  23.6 0.9 bitcast_dynamic-update-slice_fusion.17
  24.5 2.1 %fusion.14 = f32[64,1024]{1,0:T(8,128)S(1)} fusion(bf16[1,2,1024,1024]{3,2,1,0:T(8,128)(2,1)} %param.19, bf16[5,64,1024]{2,1,0:T(8,128)(2,1)S(1)} %bitcast_dynamic-update-slice_fusion.15, s32[]{:T(128)S(6)} %select_n.65), kind=kOutput, calls=%fused_computation.20 | convolution fusion | flops 134217728 | bytes 2490372 | tf_op jit(solution)/shard_map/dot_general | solution.py:36
  26.7 2.1 %fusion.201 = (bf16[64,1024]{1,0:T(8,128)(2,1)S(1)}, f32[64,1024]{1,0:T(8,128)S(1)}) fusion(f32[64,1024]{1,0:T(8,128)S(1)} %fusion.14, bf16[1,2,1024,1024]{3,2,1,0:T(8,128)(2,1)} %param.19, bf16[5,64,1024]{2,1,0:T(8,128)(2,1)S(1)} %bitcast_dynamic-update-slice_fusion.15, s32[]{:T(128)S(6)} %select_n.64, bf16[64,1024]{1,0:T(8,128)(2,1)S(1)} %copy-done.2), kind=kOutput, calls=%fused_computation.232 | convolution fusion | flops 134479872 | bytes 3014660 | tf_op jit(solution)/shard_map/dot_general | solution.py:36
  28.8 0.2 convolution_convert_fusion.1
  29.0 27.2 %all-gather = bf16[1024,128]{1,0:T(8,128)(2,1)S(1)} all-gather(bf16[64,128]{1,0:T(8,128)(2,1)S(1)} %convolution_convert_fusion.1), channel_id=2, replica_groups=mesh['parts'=2,'leaf'=16] {'leaf'}, dimensions={0}, use_global_device_ids=true | all-gather | bytes 278528 | tf_op jit(solution)/shard_map/all_gather | solution.py:59
  56.3 0.2 fusion.75
  56.8 0.6 gather_fusion.1
  57.4 0.6 gather_fusion.2
  58.0 0.2 convolution_bitcast_fusion.3
  58.2 0.2 convolution_bitcast_fusion.4
  58.4 0.4 collective-permute-start.8
  58.8 1.3 collective-permute-start.4
  60.1 2.1 %collective-permute-start.5 = (bf16[64,1024]{1,0:T(8,128)(2,1)S(1)}, bf16[64,1024]{1,0:T(8,128)(2,1)S(1)}, u32[]{:S(2)}, u32[]{:S(2)}) collective-permute-start(bf16[64,1024]{1,0:T(8,128)(2,1)S(1)} %get-tuple-element.22), channel_id=1, source_target_pairs={{0,1},{1,2},{2,3},{3,4},{4,5},{5,6},{6,7},{7,8},{8,9},{9,10},{10,1... | collective-permute-start | bytes 393224 | tf_op jit(solution)/shard_map/ppermute | solution.py:15
  62.2 1.3 collective-permute-start.6
  63.5 1.3 collective-permute-start.7
  64.8 0.6 gather_fusion
  65.4 3.7 %collective-permute-start.9 = (f32[64,128]{1,0:T(8,128)S(1)}, f32[64,128]{1,0:T(8,128)S(1)}, u32[]{:S(2)}, u32[]{:S(2)}) collective-permute-start(f32[64,128]{1,0:T(8,128)S(1)} %slice_bitcast_fusion.18), channel_id=1, source_target_pairs={{0,2},{1,3},{2,0},{3,1},{4,6},{5,7},{6,4},{7,5},{8,10},{9,11},{10,... | collective-permute-start | bytes 98312 | tf_op jit(solution)/shard_map/ppermute | solution.py:21
  69.1 0.2 convolution_bitcast_fusion.5
  69.3 3.6 %collective-permute-done.9 = f32[64,128]{1,0:T(8,128)S(1)} collective-permute-done((f32[64,128]{1,0:T(8,128)S(1)}, f32[64,128]{1,0:T(8,128)S(1)}, u32[]{:S(2)}, u32[]{:S(2)}) %collective-permute-start.9) | collective-permute-done | bytes 32800 | tf_op jit(solution)/shard_map/ppermute | solution.py:21
  72.9 0.2 fusion.154
  73.2 0.2 fusion.82
  73.4 0.2 fusion.87
  73.7 2.1 %fusion.2 = f32[64,1024]{1,0:T(8,128)S(1)} fusion(bf16[1,3,1024,1024]{3,2,1,0:T(8,128)(2,1)} %param.17, bf16[5,64,1024]{2,1,0:T(8,128)(2,1)S(1)} %bitcast_dynamic-update-slice_fusion.10, s32[]{:T(128)S(6)} %select_n.68), kind=kOutput, calls=%fused_computation.8 | convolution fusion | flops 134217728 | bytes 2490372 | tf_op jit(solution)/shard_map/dot_general | solution.py:36
  75.8 2.2 %fusion.6 = f32[64,1024]{1,0:T(8,128)S(1)} fusion(bf16[1,3,1024,1024]{3,2,1,0:T(8,128)(2,1)} %param.17, bf16[5,64,1024]{2,1,0:T(8,128)(2,1)S(1)} %bitcast_dynamic-update-slice_fusion.10, s32[]{:T(128)S(6)} %select_n.67), kind=kOutput, calls=%fused_computation.12 | convolution fusion | flops 134217728 | bytes 2490372 | tf_op jit(solution)/shard_map/dot_general | solution.py:36
  78.0 2.1 %fusion.77 = bf16[64,1024]{1,0:T(8,128)(2,1)S(1)} fusion(f32[64,1024]{1,0:T(8,128)S(1)} %fusion.87, f32[64,1024]{1,0:T(8,128)S(1)} %fusion.2, f32[64,1024]{1,0:T(8,128)S(1)} %fusion.6, bf16[1,3,1024,1024]{3,2,1,0:T(8,128)(2,1)} %param.17, bf16[64,1024]{1,0:T(8,128)(2,1)S(1)} %copy-done.2, bf16[64,1024]{1,0:T(8,128)(2,1)S(1)} %get-tuple-element.22, ...), kind=kOutput, calls=%fused_computation.55 | convolution fusion | flops 134742016 | bytes 3407876 | tf_op jit(solution)/shard_map/dot_general | solution.py:36
  80.2 3.4 %collective-permute-start.10 = (bf16[64,1024]{1,0:T(8,128)(2,1)S(1)}, bf16[64,1024]{1,0:T(8,128)(2,1)S(1)}, u32[]{:S(2)}, u32[]{:S(2)}) collective-permute-start(bf16[64,1024]{1,0:T(8,128)(2,1)S(1)} %fusion.77), channel_id=1, source_target_pairs={{0,2},{1,3},{2,4},{3,5},{4,6},{5,7},{6,8},{7,9},{8,10},{9,11},{10,... | collective-permute-start | bytes 393224 | tf_op jit(solution)/shard_map/ppermute | solution.py:15
  83.6 1.3 collective-permute-start.11
  84.9 1.3 collective-permute-start.12
  86.2 1.3 collective-permute-start.13
  87.6 2.3 %collective-permute-done.12 = bf16[64,1024]{1,0:T(8,128)(2,1)S(1)} collective-permute-done((bf16[64,1024]{1,0:T(8,128)(2,1)S(1)}, bf16[64,1024]{1,0:T(8,128)(2,1)S(1)}, u32[]{:S(2)}, u32[]{:S(2)}) %collective-permute-start.12) | collective-permute-done | bytes 131104 | tf_op jit(solution)/shard_map/ppermute | solution.py:15
  89.9 6.5 %collective-permute-done.13 = bf16[64,1024]{1,0:T(8,128)(2,1)S(1)} collective-permute-done((bf16[64,1024]{1,0:T(8,128)(2,1)S(1)}, bf16[64,1024]{1,0:T(8,128)(2,1)S(1)}, u32[]{:S(2)}, u32[]{:S(2)}) %collective-permute-start.13) | collective-permute-done | bytes 131104 | tf_op jit(solution)/shard_map/ppermute | solution.py:15
  96.4 0.5 fusion.12
  96.9 1.2 fusion.202
  98.3 19.8 %all-gather.1 = bf16[1024,128]{1,0:T(8,128)(2,1)S(1)} all-gather(bf16[64,128]{1,0:T(8,128)(2,1)S(1)} %convolution_convert_fusion), channel_id=3, replica_groups=mesh['parts'=2,'leaf'=16] {'leaf'}, dimensions={0}, use_global_device_ids=true | all-gather | bytes 278528 | tf_op jit(solution)/shard_map/all_gather | solution.py:59
  118.3 0.2 fusion.76
  118.5 0.6 gather_fusion.4
  119.3 0.6 gather_fusion.5
  119.9 0.2 convolution_bitcast_fusion
  120.1 0.2 convolution_bitcast_fusion.1
  120.3 0.4 collective-permute-start.18
  120.8 1.9 %collective-permute-start.14 = (bf16[64,1024]{1,0:T(8,128)(2,1)S(1)}, bf16[64,1024]{1,0:T(8,128)(2,1)S(1)}, u32[]{:S(2)}, u32[]{:S(2)}) collective-permute-start(bf16[64,1024]{1,0:T(8,128)(2,1)S(1)} %get-tuple-element.24), channel_id=1, source_target_pairs={{0,2},{1,3},{2,4},{3,5},{4,6},{5,7},{6,8},{7,9},{8,10},{9,11},{10,... | collective-permute-start | bytes 393224 | tf_op jit(solution)/shard_map/ppermute | solution.py:15
  122.7 1.8 %collective-permute-start.15 = (bf16[64,1024]{1,0:T(8,128)(2,1)S(1)}, bf16[64,1024]{1,0:T(8,128)(2,1)S(1)}, u32[]{:S(2)}, u32[]{:S(2)}) collective-permute-start(bf16[64,1024]{1,0:T(8,128)(2,1)S(1)} %get-tuple-element.24), channel_id=1, source_target_pairs={{0,1},{1,2},{2,3},{3,4},{4,5},{5,6},{6,7},{7,8},{8,9},{9,10},{10,1... | collective-permute-start | bytes 393224 | tf_op jit(solution)/shard_map/ppermute | solution.py:15
  124.5 1.3 collective-permute-start.16
  125.8 1.3 collective-permute-start.17
  127.1 0.6 gather_fusion.3
  127.7 3.4 %collective-permute-start.19 = (f32[64,128]{1,0:T(8,128)S(1)}, f32[64,128]{1,0:T(8,128)S(1)}, u32[]{:S(2)}, u32[]{:S(2)}) collective-permute-start(f32[64,128]{1,0:T(8,128)S(1)} %slice_bitcast_fusion.16), channel_id=1, source_target_pairs={{0,2},{1,3},{2,0},{3,1},{4,6},{5,7},{6,4},{7,5},{8,10},{9,11},{10,... | collective-permute-start | bytes 98312 | tf_op jit(solution)/shard_map/ppermute | solution.py:21
  131.1 0.2 convolution_bitcast_fusion.2
  131.3 3.6 %collective-permute-done.19 = f32[64,128]{1,0:T(8,128)S(1)} collective-permute-done((f32[64,128]{1,0:T(8,128)S(1)}, f32[64,128]{1,0:T(8,128)S(1)}, u32[]{:S(2)}, u32[]{:S(2)}) %collective-permute-start.19) | collective-permute-done | bytes 32800 | tf_op jit(solution)/shard_map/ppermute | solution.py:21
  134.9 0.2 fusion.152
  135.1 0.2 fusion.83
  135.3 0.2 fusion.84
  135.7 2.1 %fusion = f32[64,1024]{1,0:T(8,128)S(1)} fusion(bf16[1,3,1024,1024]{3,2,1,0:T(8,128)(2,1)} %param.17, bf16[5,64,1024]{2,1,0:T(8,128)(2,1)S(1)} %bitcast_dynamic-update-slice_fusion, s32[]{:T(128)S(6)} %select_n.68), kind=kOutput, calls=%fused_computation.6 | convolution fusion | flops 134217728 | bytes 2490372 | tf_op jit(solution)/shard_map/dot_general | solution.py:36
  137.7 2.1 %fusion.4 = f32[64,1024]{1,0:T(8,128)S(1)} fusion(bf16[1,3,1024,1024]{3,2,1,0:T(8,128)(2,1)} %param.17, bf16[5,64,1024]{2,1,0:T(8,128)(2,1)S(1)} %bitcast_dynamic-update-slice_fusion, s32[]{:T(128)S(6)} %select_n.67), kind=kOutput, calls=%fused_computation.10 | convolution fusion | flops 134217728 | bytes 2490372 | tf_op jit(solution)/shard_map/dot_general | solution.py:36
  139.8 2.8 %fusion.72 = f32[64,1024]{1,0:T(8,128)} fusion(f32[64,1024]{1,0:T(8,128)S(1)} %fusion.84, f32[64,1024]{1,0:T(8,128)S(1)} %fusion, f32[64,1024]{1,0:T(8,128)S(1)} %fusion.4, bf16[1,3,1024,1024]{3,2,1,0:T(8,128)(2,1)} %param.17, bf16[64,1024]{1,0:T(8,128)(2,1)S(1)} %copy-done.2, bf16[64,1024]{1,0:T(8,128)(2,1)S(1)} %get-tuple-element.24, ...), kind=kOutput, calls=%fused_computation.52 | convolution fusion | flops 134676480 | bytes 3538948 | tf_op jit(solution)/shard_map/dot_general | solution.py:36
  (61 shorter events, 1.4 us)
Async XLA Ops:
  0.6 28.1 %copy-start = (bf16[1,1024,128]{2,1,0:T(8,128)(2,1)S(1)}, bf16[1,1024,128]{2,1,0:T(8,128)(2,1)}, u32[]{:S(2)}) copy-start(bf16[1,1024,128]{2,1,0:T(8,128)(2,1)} %param.20) | copy-start | bytes 786436
  0.6 26.0 %copy-start.2 = (bf16[64,1024]{1,0:T(8,128)(2,1)S(1)}, bf16[64,1024]{1,0:T(8,128)(2,1)}, u32[]{:S(2)}) copy-start(bf16[64,1024]{1,0:T(8,128)(2,1)} %param.15) | copy-start | bytes 393220
  0.7 55.5 %copy-start.3 = (bf16[2,2,128,128]{3,2,1,0:T(8,128)(2,1)S(1)}, bf16[2,2,128,128]{3,2,1,0:T(8,128)(2,1)}, u32[]{:S(2)}) copy-start(bf16[2,2,128,128]{3,2,1,0:T(8,128)(2,1)} %param.21) | copy-start | bytes 393220
  0.7 22.8 %collective-permute-start = (bf16[64,1024]{1,0:T(8,128)(2,1)}, bf16[64,1024]{1,0:T(8,128)(2,1)S(1)}, u32[]{:S(2)}, u32[]{:S(2)}) collective-permute-start(bf16[64,1024]{1,0:T(8,128)(2,1)} %param.15), channel_id=1, source_target_pairs={{0,2},{1,3},{2,4},{3,5},{4,6},{5,7},{6,8},{7,9},{8,10},{9,11},{10,... | collective-permute-start | bytes 393224 | tf_op jit(solution)/shard_map/ppermute | solution.py:15
  5.7 17.8 %collective-permute-start.1 = (bf16[64,1024]{1,0:T(8,128)(2,1)}, bf16[64,1024]{1,0:T(8,128)(2,1)S(1)}, u32[]{:S(2)}, u32[]{:S(2)}) collective-permute-start(bf16[64,1024]{1,0:T(8,128)(2,1)} %param.15), channel_id=1, source_target_pairs={{0,1},{1,2},{2,3},{3,4},{4,5},{5,6},{6,7},{7,8},{8,9},{9,10},{10,1... | collective-permute-start | bytes 393224 | tf_op jit(solution)/shard_map/ppermute | solution.py:15
  7.2 17.3 %collective-permute-start.2 = (bf16[64,1024]{1,0:T(8,128)(2,1)}, bf16[64,1024]{1,0:T(8,128)(2,1)S(1)}, u32[]{:S(2)}, u32[]{:S(2)}) collective-permute-start(bf16[64,1024]{1,0:T(8,128)(2,1)} %param.15), channel_id=1, source_target_pairs={{1,0},{2,1},{3,2},{4,3},{5,4},{6,5},{7,6},{8,7},{9,8},{10,9},{11,1... | collective-permute-start | bytes 393224 | tf_op jit(solution)/shard_map/ppermute | solution.py:15
  8.5 16.0 %collective-permute-start.3 = (bf16[64,1024]{1,0:T(8,128)(2,1)}, bf16[64,1024]{1,0:T(8,128)(2,1)S(1)}, u32[]{:S(2)}, u32[]{:S(2)}) collective-permute-start(bf16[64,1024]{1,0:T(8,128)(2,1)} %param.15), channel_id=1, source_target_pairs={{2,0},{3,1},{4,2},{5,3},{6,4},{7,5},{8,6},{9,7},{10,8},{11,9},{12,... | collective-permute-start | bytes 393224 | tf_op jit(solution)/shard_map/ppermute | solution.py:15
  24.5 33.4 %copy-start.4 = (bf16[1,3,4,128,128]{4,3,2,1,0:T(8,128)(2,1)S(1)}, bf16[1,3,4,128,128]{4,3,2,1,0:T(8,128)(2,1)}, u32[]{:S(2)}) copy-start(bf16[1,3,4,128,128]{4,3,2,1,0:T(8,128)(2,1)} %param.23) | copy-start | bytes 1179652
  58.4 7.0 %collective-permute-start.8 = (f32[2,64,128]{2,1,0:T(8,128)S(1)}, f32[2,64,128]{2,1,0:T(8,128)S(1)}, u32[]{:S(2)}, u32[]{:S(2)}) collective-permute-start(f32[2,64,128]{2,1,0:T(8,128)S(1)} %pad_maximum_fusion), channel_id=1, source_target_pairs={{0,1},{1,0},{2,3},{3,2},{4,5},{5,4},{6,7},{7,6},{8,9},{9,8},{10,11... | collective-permute-start | bytes 196616 | tf_op jit(solution)/shard_map/ppermute | solution.py:21
  58.8 14.8 %collective-permute-start.4 = (bf16[64,1024]{1,0:T(8,128)(2,1)S(1)}, bf16[64,1024]{1,0:T(8,128)(2,1)S(1)}, u32[]{:S(2)}, u32[]{:S(2)}) collective-permute-start(bf16[64,1024]{1,0:T(8,128)(2,1)S(1)} %get-tuple-element.22), channel_id=1, source_target_pairs={{0,2},{1,3},{2,4},{3,5},{4,6},{5,7},{6,8},{7,9},{8,10},{9,11},{10,... | collective-permute-start | bytes 393224 | tf_op jit(solution)/shard_map/ppermute | solution.py:15
  60.1 13.5 %collective-permute-start.5 = (bf16[64,1024]{1,0:T(8,128)(2,1)S(1)}, bf16[64,1024]{1,0:T(8,128)(2,1)S(1)}, u32[]{:S(2)}, u32[]{:S(2)}) collective-permute-start(bf16[64,1024]{1,0:T(8,128)(2,1)S(1)} %get-tuple-element.22), channel_id=1, source_target_pairs={{0,1},{1,2},{2,3},{3,4},{4,5},{5,6},{6,7},{7,8},{8,9},{9,10},{10,1... | collective-permute-start | bytes 393224 | tf_op jit(solution)/shard_map/ppermute | solution.py:15
  62.2 11.5 %collective-permute-start.6 = (bf16[64,1024]{1,0:T(8,128)(2,1)S(1)}, bf16[64,1024]{1,0:T(8,128)(2,1)S(1)}, u32[]{:S(2)}, u32[]{:S(2)}) collective-permute-start(bf16[64,1024]{1,0:T(8,128)(2,1)S(1)} %get-tuple-element.22), channel_id=1, source_target_pairs={{1,0},{2,1},{3,2},{4,3},{5,4},{6,5},{7,6},{8,7},{9,8},{10,9},{11,1... | collective-permute-start | bytes 393224 | tf_op jit(solution)/shard_map/ppermute | solution.py:15
  63.5 10.2 %collective-permute-start.7 = (bf16[64,1024]{1,0:T(8,128)(2,1)S(1)}, bf16[64,1024]{1,0:T(8,128)(2,1)S(1)}, u32[]{:S(2)}, u32[]{:S(2)}) collective-permute-start(bf16[64,1024]{1,0:T(8,128)(2,1)S(1)} %get-tuple-element.22), channel_id=1, source_target_pairs={{2,0},{3,1},{4,2},{5,3},{6,4},{7,5},{8,6},{9,7},{10,8},{11,9},{12,... | collective-permute-start | bytes 393224 | tf_op jit(solution)/shard_map/ppermute | solution.py:15
  65.4 7.6 %collective-permute-start.9 = (f32[64,128]{1,0:T(8,128)S(1)}, f32[64,128]{1,0:T(8,128)S(1)}, u32[]{:S(2)}, u32[]{:S(2)}) collective-permute-start(f32[64,128]{1,0:T(8,128)S(1)} %slice_bitcast_fusion.18), channel_id=1, source_target_pairs={{0,2},{1,3},{2,0},{3,1},{4,6},{5,7},{6,4},{7,5},{8,10},{9,11},{10,... | collective-permute-start | bytes 98312 | tf_op jit(solution)/shard_map/ppermute | solution.py:21
  75.8 20.6 %copy-start.1 = (bf16[1,2,1024,1024]{3,2,1,0:T(8,128)(2,1)S(1)}, bf16[1,2,1024,1024]{3,2,1,0:T(8,128)(2,1)}, u32[]{:S(2)}) copy-start(bf16[1,2,1024,1024]{3,2,1,0:T(8,128)(2,1)} %param.19) | copy-start | bytes 12582916
  80.2 7.3 %collective-permute-start.10 = (bf16[64,1024]{1,0:T(8,128)(2,1)S(1)}, bf16[64,1024]{1,0:T(8,128)(2,1)S(1)}, u32[]{:S(2)}, u32[]{:S(2)}) collective-permute-start(bf16[64,1024]{1,0:T(8,128)(2,1)S(1)} %fusion.77), channel_id=1, source_target_pairs={{0,2},{1,3},{2,4},{3,5},{4,6},{5,7},{6,8},{7,9},{8,10},{9,11},{10,... | collective-permute-start | bytes 393224 | tf_op jit(solution)/shard_map/ppermute | solution.py:15
  83.6 3.9 %collective-permute-start.11 = (bf16[64,1024]{1,0:T(8,128)(2,1)S(1)}, bf16[64,1024]{1,0:T(8,128)(2,1)S(1)}, u32[]{:S(2)}, u32[]{:S(2)}) collective-permute-start(bf16[64,1024]{1,0:T(8,128)(2,1)S(1)} %fusion.77), channel_id=1, source_target_pairs={{0,1},{1,2},{2,3},{3,4},{4,5},{5,6},{6,7},{7,8},{8,9},{9,10},{10,1... | collective-permute-start | bytes 393224 | tf_op jit(solution)/shard_map/ppermute | solution.py:15
  84.9 5.0 %collective-permute-start.12 = (bf16[64,1024]{1,0:T(8,128)(2,1)S(1)}, bf16[64,1024]{1,0:T(8,128)(2,1)S(1)}, u32[]{:S(2)}, u32[]{:S(2)}) collective-permute-start(bf16[64,1024]{1,0:T(8,128)(2,1)S(1)} %fusion.77), channel_id=1, source_target_pairs={{1,0},{2,1},{3,2},{4,3},{5,4},{6,5},{7,6},{8,7},{9,8},{10,9},{11,1... | collective-permute-start | bytes 393224 | tf_op jit(solution)/shard_map/ppermute | solution.py:15
  86.2 10.2 %collective-permute-start.13 = (bf16[64,1024]{1,0:T(8,128)(2,1)S(1)}, bf16[64,1024]{1,0:T(8,128)(2,1)S(1)}, u32[]{:S(2)}, u32[]{:S(2)}) collective-permute-start(bf16[64,1024]{1,0:T(8,128)(2,1)S(1)} %fusion.77), channel_id=1, source_target_pairs={{2,0},{3,1},{4,2},{5,3},{6,4},{7,5},{8,6},{9,7},{10,8},{11,9},{12,... | collective-permute-start | bytes 393224 | tf_op jit(solution)/shard_map/ppermute | solution.py:15
  120.3 7.3 %collective-permute-start.18 = (f32[2,64,128]{2,1,0:T(8,128)S(1)}, f32[2,64,128]{2,1,0:T(8,128)S(1)}, u32[]{:S(2)}, u32[]{:S(2)}) collective-permute-start(f32[2,64,128]{2,1,0:T(8,128)S(1)} %pad_maximum_fusion.1), channel_id=1, source_target_pairs={{0,1},{1,0},{2,3},{3,2},{4,5},{5,4},{6,7},{7,6},{8,9},{9,8},{10,11... | collective-permute-start | bytes 196616 | tf_op jit(solution)/shard_map/ppermute | solution.py:21
  120.8 14.8 %collective-permute-start.14 = (bf16[64,1024]{1,0:T(8,128)(2,1)S(1)}, bf16[64,1024]{1,0:T(8,128)(2,1)S(1)}, u32[]{:S(2)}, u32[]{:S(2)}) collective-permute-start(bf16[64,1024]{1,0:T(8,128)(2,1)S(1)} %get-tuple-element.24), channel_id=1, source_target_pairs={{0,2},{1,3},{2,4},{3,5},{4,6},{5,7},{6,8},{7,9},{8,10},{9,11},{10,... | collective-permute-start | bytes 393224 | tf_op jit(solution)/shard_map/ppermute | solution.py:15
  122.7 12.9 %collective-permute-start.15 = (bf16[64,1024]{1,0:T(8,128)(2,1)S(1)}, bf16[64,1024]{1,0:T(8,128)(2,1)S(1)}, u32[]{:S(2)}, u32[]{:S(2)}) collective-permute-start(bf16[64,1024]{1,0:T(8,128)(2,1)S(1)} %get-tuple-element.24), channel_id=1, source_target_pairs={{0,1},{1,2},{2,3},{3,4},{4,5},{5,6},{6,7},{7,8},{8,9},{9,10},{10,1... | collective-permute-start | bytes 393224 | tf_op jit(solution)/shard_map/ppermute | solution.py:15
  124.5 11.1 %collective-permute-start.16 = (bf16[64,1024]{1,0:T(8,128)(2,1)S(1)}, bf16[64,1024]{1,0:T(8,128)(2,1)S(1)}, u32[]{:S(2)}, u32[]{:S(2)}) collective-permute-start(bf16[64,1024]{1,0:T(8,128)(2,1)S(1)} %get-tuple-element.24), channel_id=1, source_target_pairs={{1,0},{2,1},{3,2},{4,3},{5,4},{6,5},{7,6},{8,7},{9,8},{10,9},{11,1... | collective-permute-start | bytes 393224 | tf_op jit(solution)/shard_map/ppermute | solution.py:15
  125.8 9.9 %collective-permute-start.17 = (bf16[64,1024]{1,0:T(8,128)(2,1)S(1)}, bf16[64,1024]{1,0:T(8,128)(2,1)S(1)}, u32[]{:S(2)}, u32[]{:S(2)}) collective-permute-start(bf16[64,1024]{1,0:T(8,128)(2,1)S(1)} %get-tuple-element.24), channel_id=1, source_target_pairs={{2,0},{3,1},{4,2},{5,3},{6,4},{7,5},{8,6},{9,7},{10,8},{11,9},{12,... | collective-permute-start | bytes 393224 | tf_op jit(solution)/shard_map/ppermute | solution.py:15
  127.7 7.2 %collective-permute-start.19 = (f32[64,128]{1,0:T(8,128)S(1)}, f32[64,128]{1,0:T(8,128)S(1)}, u32[]{:S(2)}, u32[]{:S(2)}) collective-permute-start(f32[64,128]{1,0:T(8,128)S(1)} %slice_bitcast_fusion.16), channel_id=1, source_target_pairs={{0,2},{1,3},{2,0},{3,1},{4,6},{5,7},{6,4},{7,5},{8,10},{9,11},{10,... | collective-permute-start | bytes 98312 | tf_op jit(solution)/shard_map/ppermute | solution.py:21
where the time goes:
time: 144 us; the launch traced here: 143 us
  blocking collectives  47 us (33%)
  starting transfers between devices  36.5 us (25%)
  matrix products  23.3 us (16%)
  waiting for transfers between devices  16.1 us (11%)
  between operations  10.9 us (8%)
  local copies, waits for them, and re-layouts  6.68 us (5%)
  other arithmetic  2.07 us (1%)
    all_gather x2, blocking collectives, far_term(): table_zero = lax.all_gather(coeff_zero[None], 'leaf', axis=0, tiled=True)  47 us
    ppermute x16, starting transfers between devices, from_behind(): lax.ppermute(value, axis, [(source, source + steps) for source in range(f...  28.6 us
    dot_general x10, matrix products, apply_slots(): jnp.dot(chosen, blocks[slot_index], preferred_element_type=jnp.float32)  19.3 us
    ppermute x16, waiting for transfers between devices, from_behind(): lax.ppermute(value, axis, [(source, source + steps) for source in range(f...  8.85 us
    ppermute x4, starting transfers between devices, partner(): return lax.ppermute(value, axis, pairs)  7.94 us
    ppermute x4, waiting for transfers between devices, partner(): return lax.ppermute(value, axis, pairs)  7.25 us
    gather x6, local copies, waits for them, and re-layouts, far_term(): chosen = jnp.take(coeff_table, couple_list[0, tree_level], axis=0)  3.38 us
  transfers between devices with their start and end apart: 20, of which 4 were waited for; matrix products, arithmetic and copies ran while one was open for 6% of the time, Pallas kernels for 0%

commit v1 on v0

v1 whole, which is shorter than its diff:
```python
import functools

import jax
import jax.numpy as jnp
from jax import lax
from jax.experimental import pallas as pl
from jax.experimental.pallas import tpu as pltpu
from jax.sharding import PartitionSpec as P

REACH = 2
CHUNKS = 4
EXCHANGES = 4
OWN_SIB, OWN_PAIR, FWD_QUAD, FWD_SIB = range(4)
F32 = jnp.float32
BF16 = jnp.bfloat16


def mm(a, b):
    return jnp.dot(a, b, preferred_element_type=F32)


def mm_t(a, b):
    return lax.dot_general(a, b, (((1,), (1,)), ((), ())), preferred_element_type=F32)


def kernel(
    count,
    near_list,
    inverse_list,
    couple_list,
    sides_hbm,
    near_hbm,
    inverse_hbm,
    bases_hbm,
    transfers_hbm,
    couple_hbm,
    sol_ref,
    res_ref,
    *scratch,
):
    windows = [scratch[e * CHUNKS : (e + 1) * CHUNKS] for e in range(EXCHANGES)]
    (
        tables_a,
        tables_b,
        got_a,
        got_b,
        mine_a,
        mine_b,
        level_one,
        level_two,
        near,
        inverse,
        bases,
        transfers,
        couple,
        acc,
        load_sem,
        sides_sem,
        send_sem,
        recv_sem,
        far_send,
        far_recv,
        step_send,
        step_recv,
    ) = scratch[EXCHANGES * CHUNKS :]
    tables = (tables_a, tables_b)
    got = (got_a, got_b)
    mine = (mine_a, mine_b)
    quads = count // 4
    rows, cols = sol_ref.shape
    width = cols // CHUNKS

    me = lax.axis_index("leaf")
    core = me % 2
    odd = me // 2 % 2
    member = me % 4
    quad = me // 4
    sibling = me + 1 - 2 * core
    pair = me + 2 - 4 * odd
    across = pair + 1 - 2 * core
    pair_slot = 4 - 4 * odd
    fwd_slot = 4 * odd
    pair_dst_slot = 4 * odd
    fwd_to = me + 4 - 8 * odd
    fwd_out = (fwd_to >= 0) & (fwd_to < count)
    fwd_from = me - 4 + 8 * odd
    fwd_in = (fwd_from >= 0) & (fwd_from < count)
    same = core == odd

    sides_loads = []
    for c in range(CHUNKS):
        load = pltpu.make_async_copy(
            sides_hbm.at[:, pl.ds(c * width, width)], windows[0][c].at[2], sides_sem.at[c]
        )
        load.start()
        sides_loads.append(load)
    loads = {}
    pieces = []
    for s in range(inverse.shape[0]):
        pieces.append(("inverse%d" % s, inverse_hbm.at[0, s], inverse.at[s]))
    pieces.append(("bases", bases_hbm.at[0], bases))
    pieces.append(("transfers", transfers_hbm, transfers))
    pieces.append(("couple", couple_hbm.at[0], couple))
    for s in range(near.shape[0]):
        pieces.append(("near%d" % s, near_hbm.at[0, s], near.at[s]))
    for index, (name, source, target) in enumerate(pieces):
        loads[name] = pltpu.make_async_copy(source, target, load_sem.at[index])
        loads[name].start()

    def wait_load(*names):
        for name in names:
            if name in loads:
                loads.pop(name).wait()

    barrier = pltpu.get_barrier_semaphore()
    partners = [sibling, pair, across]
    partners += [(quad + k) % quads * 4 + member for k in range(1, quads)]
    for other in partners:
        pl.semaphore_signal(
            barrier, inc=1, device_id={"leaf": other}, device_id_type=pl.DeviceIdType.MESH
        )
    pl.semaphore_wait(barrier, len(partners))

    unsent = []

    def remote(src, dst, ssem, rsem, to):
        return pltpu.make_async_remote_copy(
            src_ref=src,
            dst_ref=dst,
            send_sem=ssem,
            recv_sem=rsem,
            device_id={"leaf": to},
            device_id_type=pl.DeviceIdType.MESH,
        )

    def vector_copy(e, c, kind):
        win = windows[e][c]
        if kind == OWN_SIB:
            src, dst, to = 2, 1 + 2 * core, sibling
            dst = jnp.where(core == 0, 1, 3)
        elif kind == OWN_PAIR:
            src, dst, to = 2, pair_dst_slot, pair
        elif kind == FWD_QUAD:
            src, dst, to = pair_slot, fwd_slot, fwd_to
        else:
            src, dst, to = 4 - 4 * core, 3 - 2 * core, sibling
        return remote(
            win.at[src], win.at[dst], send_sem.at[e, kind, c], recv_sem.at[e, kind, c], to
        )

    def start(e, c, kind, pred=None):
        if pred is None:
            vector_copy(e, c, kind).start()
        else:
            pl.when(pred)(lambda: vector_copy(e, c, kind).start())

    def wait_recv(e, c, kind, pred=None):
        if pred is None:
            vector_copy(e, c, kind).wait_recv()
        else:
            pl.when(pred)(lambda: vector_copy(e, c, kind).wait_recv())

    def send_own(e, c):
        start(e, c, OWN_PAIR)
        start(e, c, OWN_SIB)

    def relay(e, c):
        wait_recv(e, c, OWN_PAIR)
        start(e, c, FWD_QUAD, fwd_out)
        start(e, c, FWD_SIB, same)
        wait_recv(e, c, FWD_QUAD, fwd_in)
        start(e, c, FWD_SIB, jnp.logical_not(same) & fwd_in)

    def arrive(e, c):
        wait_recv(e, c, OWN_SIB)
        wait_recv(e, c, FWD_SIB, jnp.logical_not(same) | fwd_in)

    def drain(e):
        for c in range(CHUNKS):
            vector_copy(e, c, OWN_PAIR).wait_send()
            vector_copy(e, c, OWN_SIB).wait_send()
            pl.when(fwd_out)(lambda c=c: vector_copy(e, c, FWD_QUAD).wait_send())
            pl.when(same | fwd_in)(lambda c=c: vector_copy(e, c, FWD_SIB).wait_send())

    def own(e):
        return jnp.concatenate([windows[e][c][2] for c in range(CHUNKS)], axis=1)

    def put_own(e, value):
        for c in range(CHUNKS):
            windows[e][c][2] = value[:, c * width : (c + 1) * width].astype(BF16)
            send_own(e, c)

    def within(leaf):
        return jnp.clip(leaf - me + REACH, 0, 2 * REACH)

    near_at = [within(near_list[0, s]) for s in range(near.shape[0])]
    inverse_at = [within(inverse_list[0, s]) for s in range(inverse.shape[0])]

    def slots(e, c, at, blocks, label):
        arrive(e, c)
        total = None
        for s, position in enumerate(at):
            wait_load("%s%d" % (label, s))
            chosen = windows[e][c][position]
            term = mm(chosen, blocks[s, c * width : (c + 1) * width, :])
            total = term if total is None else total + term
        if c == 0:
            acc[...] = total
        else:
            acc[...] += total

    def blocksum(e, at, blocks, label):
        relay(e, 0)
        for c in range(CHUNKS):
            if c + 1 < CHUNKS:
                relay(e, c + 1)
            slots(e, c, at, blocks, label)

    def far_along(a, k):
        ref = tables[a].at[member, quad]
        return remote(ref, ref, far_send.at[a, k], far_recv.at[a, k], (quad + k) % quads * 4 + member)

    def far_step(a, kind):
        table = tables[a]
        if kind == 0:
            ref, to, dst = table.at[member], pair, None
        elif kind == 1:
            ref, to, dst = table.at[member], sibling, None
        elif kind == 2:
            ref, to, dst = table.at[pair % 4], sibling, None
        elif kind == 3:
            ref, to, dst = mine[a], sibling, got[a].at[pl.ds(0, 2)]
        elif kind == 4:
            ref, to, dst = mine[a].at[1], pair, got[a].at[2]
        else:
            ref, to, dst = mine[a].at[1], across, got[a].at[3]
        return remote(
            ref, ref if dst is None else dst, step_send.at[a, kind], step_recv.at[a, kind], to
        )

    def far_begin(a, e):
        wait_load("bases")
        tables[a][member, quad] = mm(own(e), bases[...]).astype(BF16)
        for k in range(1, quads):
            far_along(a, k).start()

    def far_mid(a):
        for k in range(1, quads):
            far_along(a, k).wait_recv()
        far_step(a, 0).start()
        far_step(a, 1).start()

    def far_late(a):
        far_step(a, 0).wait_recv()
        far_step(a, 2).start()

    def far_couple(a):
        table = tables[a]
        wait_load("transfers", "couple")
        far_step(a, 1).wait_recv()
        far_step(a, 2).wait_recv()
        rank = table.shape[-1]
        flat = (quads * rows, rank)
        for parity in range(2):
            lifted = mm(table[2 * parity].reshape(flat), transfers[0, 0])
            lifted = lifted + mm(table[2 * parity + 1].reshape(flat), transfers[0, 1])
            level_one[parity] = lifted.astype(BF16).reshape(quads, rows, rank)
        lifted = mm(level_one[0].reshape(flat), transfers[1, 0])
        lifted = lifted + mm(level_one[1].reshape(flat), transfers[1, 1])
        level_two[...] = lifted.astype(BF16).reshape(quads, rows, rank)
        fields = []
        for level in range(3):
            total = None
            for k in range(couple.shape[1]):
                at = couple_list[level, 0, k]
                if level == 0:
                    chosen = table[at % 4, at // 4]
                elif level == 1:
                    chosen = level_one[at % 2, at // 2]
                else:
                    chosen = level_two[at]
                term = mm(chosen, couple[level, k])
                total = term if total is None else total + term
            fields.append(total)
        mine[a][0] = fields[1].astype(BF16)
        mine[a][1] = fields[2].astype(BF16)
        for kind in (4, 5, 3):
            far_step(a, kind).start()
        return fields

    def far_end(a, fields):
        for kind in (3, 4, 5):
            far_step(a, kind).wait_recv()
        pair_one = fields[1] + got[a][0].astype(F32)
        quad_sum = fields[2] + got[a][1].astype(F32)
        quad_sum = quad_sum + got[a][2].astype(F32) + got[a][3].astype(F32)
        down = pair_one + mm_t(quad_sum.astype(BF16), transfers[1, odd])
        field = fields[0] + mm_t(down.astype(BF16), transfers[0, core])
        return mm_t(field.astype(BF16), bases[...])

    def far_drain(a):
        for k in range(1, quads):
            far_along(a, k).wait_send()
        for kind in range(6):
            far_step(a, kind).wait_send()

    def operate(e, a):
        far_begin(a, e)
        relay(e, 0)
        relay(e, 1)
        far_mid(a)
        slots(e, 0, near_at, near, "near")
        relay(e, 2)
        slots(e, 1, near_at, near, "near")
        relay(e, 3)
        far_late(a)
        slots(e, 2, near_at, near, "near")
        fields = far_couple(a)
        slots(e, 3, near_at, near, "near")
        return own(e).astype(F32) + acc[...] + far_end(a, fields)

    for c in range(CHUNKS):
        sides_loads[c].wait()
        send_own(0, c)
    blocksum(0, inverse_at, inverse, "inverse")
    first = own(0).astype(F32) + acc[...]
    put_own(1, first)
    sol_ref[...] = first
    put_own(2, own(0).astype(F32) - operate(1, 0))
    blocksum(2, inverse_at, inverse, "inverse")
    second = sol_ref[...] + (own(2).astype(F32) + acc[...])
    put_own(3, second)
    sol_ref[...] = second
    res_ref[...] = own(0).astype(F32) - operate(3, 1)
    for e in range(EXCHANGES):
        drain(e)
    for a in range(2):
        far_drain(a)


def shards(
    count,
    right_sides,
    near_list,
    near_blocks,
    inverse_list,
    inverse_blocks,
    leaf_bases,
    transfers,
    couple_list,
    couple_blocks,
):
    rows, cols = right_sides.shape
    rank = leaf_bases.shape[-1]
    quads = count // 4
    width = cols // CHUNKS
    window = pltpu.VMEM((2 * REACH + 1, rows, width), BF16)
    table = pltpu.VMEM((4, quads, rows, rank), BF16)
    got = pltpu.VMEM((4, rows, rank), BF16)
    mine = pltpu.VMEM((2, rows, rank), BF16)
    dma = pltpu.SemaphoreType.DMA
    loads = near_blocks.shape[1] + inverse_blocks.shape[1] + 3
    scratch = [window] * (EXCHANGES * CHUNKS) + [
        table,
        table,
        got,
        got,
        mine,
        mine,
        pltpu.VMEM((2, quads, rows, rank), BF16),
        pltpu.VMEM((quads, rows, rank), BF16),
        pltpu.VMEM(near_blocks.shape[1:], BF16),
        pltpu.VMEM(inverse_blocks.shape[1:], BF16),
        pltpu.VMEM(leaf_bases.shape[1:], BF16),
        pltpu.VMEM(transfers.shape, BF16),
        pltpu.VMEM(couple_blocks.shape[1:], BF16),
        pltpu.VMEM((rows, cols), F32),
        dma((loads,)),
        dma((CHUNKS,)),
        dma((EXCHANGES, 4, CHUNKS)),
        dma((EXCHANGES, 4, CHUNKS)),
        dma((2, quads)),
        dma((2, quads)),
        dma((2, 6)),
        dma((2, 6)),
    ]
    smem = pl.BlockSpec(memory_space=pltpu.SMEM)
    hbm = pl.BlockSpec(memory_space=pl.ANY)
    vmem = pl.BlockSpec(memory_space=pltpu.VMEM)
    out = jax.ShapeDtypeStruct((rows, cols), F32)
    return pl.pallas_call(
        functools.partial(kernel, count),
        out_shape=(out, out),
        in_specs=[smem] * 3 + [hbm] * 6,
        out_specs=(vmem, vmem),
        scratch_shapes=scratch,
        compiler_params=pltpu.CompilerParams(
            collective_id=0, has_side_effects=True, vmem_limit_bytes=67_043_328
        ),
    )(
        near_list,
        inverse_list,
        jnp.transpose(couple_list, (1, 0, 2)),
        right_sides,
        near_blocks,
        inverse_blocks,
        leaf_bases,
        transfers,
        couple_blocks,
    )


def solution(mesh):
    return jax.shard_map(
        functools.partial(shards, mesh.shape["leaf"]),
        mesh=mesh,
        in_specs=(
            P("parts", "leaf"),
            P(("parts", "leaf"), None),
            P(("parts", "leaf"), None, None, None),
            P(("parts", "leaf"), None),
            P(("parts", "leaf"), None, None, None),
            P(("parts", "leaf"), None, None),
            P(),
            P(("parts", "leaf"), None, None),
            P(("parts", "leaf"), None, None, None, None),
        ),
        out_specs=(P("parts", "leaf"), P("parts", "leaf")),
        check_vma=False,
    )
```

time: 144 us -> 75.6 us (0.52)
  Pallas kernels: 0 us -> 71.4 us
  blocking collectives: 47 us -> 0 us
  starting transfers between devices: 36.5 us -> 0 us
  matrix products: 23.3 us -> 0 us
  waiting for transfers between devices: 16.1 us -> 0 us
  between operations: 10.9 us -> 0.64 us
  local copies, waits for them, and re-layouts: 6.68 us -> 3.34 us
  other arithmetic: 2.07 us -> 0 us
    pallas_call x0 -> x1, Pallas kernels: none -> 71.4 us  [shards(): pl.pallas_call(functools.partial(kernel, count), out_shape=(out, out), in...]
    all_gather x2 -> x0, blocking collectives: 47 us -> none  [far_term(): table_zero = lax.all_gather(coeff_zero[None], 'leaf', axis=0, tiled=True)]
    ppermute x20 -> x0, starting transfers between devices: 36.5 us -> none  [the longest x16 28.6 us: from_behind(): lax.ppermute(value, axis, [(source, source + steps) for source in range(f...]
    dot_general x32 -> x0, matrix products: 23.3 us -> none  [the longest x10 19.3 us: apply_slots(): jnp.dot(chosen, blocks[slot_index], preferred_element_type=jnp.float32)]
    ppermute x20 -> x0, waiting for transfers between devices: 16.1 us -> none  [the longest x16 8.85 us: from_behind(): lax.ppermute(value, axis, [(source, source + steps) for source in range(f...]
    gather x6 -> x0, local copies, waits for them, and re-layouts: 3.38 us -> none  [far_term(): chosen = jnp.take(coeff_table, couple_list[0, tree_level], axis=0)]
    unnamed x26 -> x2, local copies, waits for them, and re-layouts: 1.11 us -> 3.34 us
    slice x3 -> x0, local copies, waits for them, and re-layouts: 2.13 us -> none  [the longest x2 1.25 us: apply_slots(): relative[slot_index]]
  transfers between devices with their start and end apart: 20 -> 0, of which waited for: 4 -> 0; matrix products, arithmetic and copies ran while one was open for 6% -> 0% of each run, Pallas kernels for 0% -> 0%
where the time goes in v1:
time: 75.6 us; the launch traced here: 75.4 us
  Pallas kernels  71.4 us (94%)
  local copies, waits for them, and re-layouts  3.34 us (4%)
    pallas_call x1, Pallas kernels, shards(): pl.pallas_call(functools.partial(kernel, count), out_shape=(out, out), in...  71.4 us
    unnamed x2, local copies, waits for them, and re-layouts  3.34 us

profile of v1, /device:TPU:0, one launch (start us, length us, event | category | flops | bytes accessed | tf_op | source)
XLA Modules:
  0.0 75.4 jit_solution(10449888646391763356)
XLA Ops:
  0.6 71.4 %shard_map.104 = (f32[64,1024]{1,0:T(8,128)}, f32[64,1024]{1,0:T(8,128)}) custom-call(s32[1,3]{1,0:T(1,128)} %near_list.1, s32[1,2]{1,0:T(1,128)} %inverse_list.1, s32[3,1,4]{2,1,0:T(1,128)} %bitcast.1, bf16[64,1024]{1,0:T(8,128)(2,1)} %sides_hbm.1, bf16[1,3,1024,1024]{3,2,1,0:T(8,128)(2,1)} %near_hbm.1, bf16[1,2,1024,1024]{3,2,1,0:T(8,128)(2,1)} %inverse_hbm.1, ...), custom_call_target="tpu_custom_call" | custom-call | tf_op jit(solution)/shard_map/pallas_call | solution.py:391
  72.0 1.7 %copy.13 = f32[64,1024]{1,0:T(8,128)} copy(f32[64,1024]{1,0:T(8,128)} %get-tuple-element.4) | data formatting | bytes 524288
  73.7 1.7 %copy.14 = f32[64,1024]{1,0:T(8,128)} copy(f32[64,1024]{1,0:T(8,128)} %get-tuple-element.5) | data formatting | bytes 524288

commit v2 on v1

--- a/solution.py
+++ b/solution.py
@@ -60,6 +60,8 @@
         recv_sem,
         far_send,
         far_recv,
+        row_send,
+        row_recv,
         step_send,
         step_recv,
     ) = scratch[EXCHANGES * CHUNKS :]
@@ -168,6 +170,8 @@
         wait_recv(e, c, OWN_PAIR)
         start(e, c, FWD_QUAD, fwd_out)
         start(e, c, FWD_SIB, same)
+
+    def pass_on(e, c):
         wait_recv(e, c, FWD_QUAD, fwd_in)
         start(e, c, FWD_SIB, jnp.logical_not(same) & fwd_in)
 
@@ -210,55 +214,57 @@
             acc[...] += total
 
     def blocksum(e, at, blocks, label):
-        relay(e, 0)
+        for c in range(CHUNKS):
+            relay(e, c)
+        pass_on(e, 0)
         for c in range(CHUNKS):
             if c + 1 < CHUNKS:
-                relay(e, c + 1)
+                pass_on(e, c + 1)
             slots(e, c, at, blocks, label)
 
     def far_along(a, k):
         ref = tables[a].at[member, quad]
         return remote(ref, ref, far_send.at[a, k], far_recv.at[a, k], (quad + k) % quads * 4 + member)
 
+    def far_spread(a, kind, k):
+        ref = tables[a].at[pair % 4 if kind == 2 else member, (quad - k + quads) % quads]
+        to = pair if kind == 0 else sibling
+        return remote(ref, ref, row_send.at[a, kind, k], row_recv.at[a, kind, k], to)
+
     def far_step(a, kind):
-        table = tables[a]
         if kind == 0:
-            ref, to, dst = table.at[member], pair, None
+            ref, to, dst = mine[a], sibling, got[a].at[pl.ds(0, 2)]
         elif kind == 1:
-            ref, to, dst = table.at[member], sibling, None
-        elif kind == 2:
-            ref, to, dst = table.at[pair % 4], sibling, None
-        elif kind == 3:
-            ref, to, dst = mine[a], sibling, got[a].at[pl.ds(0, 2)]
-        elif kind == 4:
             ref, to, dst = mine[a].at[1], pair, got[a].at[2]
         else:
             ref, to, dst = mine[a].at[1], across, got[a].at[3]
-        return remote(
-            ref, ref if dst is None else dst, step_send.at[a, kind], step_recv.at[a, kind], to
-        )
+        return remote(ref, dst, step_send.at[a, kind], step_recv.at[a, kind], to)
 
     def far_begin(a, e):
         wait_load("bases")
         tables[a][member, quad] = mm(own(e), bases[...]).astype(BF16)
         for k in range(1, quads):
             far_along(a, k).start()
+        far_spread(a, 0, 0).start()
+        far_spread(a, 1, 0).start()
 
     def far_mid(a):
         for k in range(1, quads):
             far_along(a, k).wait_recv()
-        far_step(a, 0).start()
-        far_step(a, 1).start()
+            far_spread(a, 0, k).start()
+            far_spread(a, 1, k).start()
 
     def far_late(a):
-        far_step(a, 0).wait_recv()
-        far_step(a, 2).start()
+        for k in range(quads):
+            far_spread(a, 0, k).wait_recv()
+            far_spread(a, 2, k).start()
 
     def far_couple(a):
         table = tables[a]
         wait_load("transfers", "couple")
-        far_step(a, 1).wait_recv()
-        far_step(a, 2).wait_recv()
+        for k in range(quads):
+            far_spread(a, 1, k).wait_recv()
+            far_spread(a, 2, k).wait_recv()
         rank = table.shape[-1]
         flat = (quads * rows, rank)
         for parity in range(2):
@@ -284,12 +290,12 @@
             fields.append(total)
         mine[a][0] = fields[1].astype(BF16)
         mine[a][1] = fields[2].astype(BF16)
-        for kind in (4, 5, 3):
+        for kind in (1, 2, 0):
             far_step(a, kind).start()
         return fields
 
     def far_end(a, fields):
-        for kind in (3, 4, 5):
+        for kind in (0, 1, 2):
             far_step(a, kind).wait_recv()
         pair_one = fields[1] + got[a][0].astype(F32)
         quad_sum = fields[2] + got[a][1].astype(F32)
@@ -301,22 +307,26 @@
     def far_drain(a):
         for k in range(1, quads):
             far_along(a, k).wait_send()
-        for kind in range(6):
+        for kind in range(3):
             far_step(a, kind).wait_send()
+            for k in range(quads):
+                far_spread(a, kind, k).wait_send()
 
     def operate(e, a):
         far_begin(a, e)
-        relay(e, 0)
-        relay(e, 1)
+        for c in range(CHUNKS - 1):
+            relay(e, c)
         far_mid(a)
-        slots(e, 0, near_at, near, "near")
-        relay(e, 2)
-        slots(e, 1, near_at, near, "near")
-        relay(e, 3)
-        far_late(a)
-        slots(e, 2, near_at, near, "near")
+        relay(e, CHUNKS - 1)
+        for c in range(CHUNKS - 1):
+            pass_on(e, c)
+            if c + 1 == CHUNKS // 2:
+                far_late(a)
+        for c in range(CHUNKS - 1):
+            slots(e, c, near_at, near, "near")
+        pass_on(e, CHUNKS - 1)
         fields = far_couple(a)
-        slots(e, 3, near_at, near, "near")
+        slots(e, CHUNKS - 1, near_at, near, "near")
         return own(e).astype(F32) + acc[...] + far_end(a, fields)
 
     for c in range(CHUNKS):
@@ -381,8 +391,10 @@
         dma((EXCHANGES, 4, CHUNKS)),
         dma((2, quads)),
         dma((2, quads)),
-        dma((2, 6)),
-        dma((2, 6)),
+        dma((2, 3, quads)),
+        dma((2, 3, quads)),
+        dma((2, 3)),
+        dma((2, 3)),
     ]
     smem = pl.BlockSpec(memory_space=pltpu.SMEM)
     hbm = pl.BlockSpec(memory_space=pl.ANY)

time: 75.6 us -> 54.6 us (0.72)
  Pallas kernels: 71.4 us -> 50.5 us
    pallas_call x1, Pallas kernels: 71.4 us -> 50.5 us  [shards(): pl.pallas_call(functools.partial(kernel, count), out_shape=(out, out), in...]
where the time goes in v2:
time: 54.6 us; the launch traced here: 54.4 us
  Pallas kernels  50.5 us (92%)
  local copies, waits for them, and re-layouts  3.34 us (6%)
  between operations  0.64 us (1%)
    pallas_call x1, Pallas kernels, shards(): pl.pallas_call(functools.partial(kernel, count), out_shape=(out, out), in...  50.5 us
    unnamed x2, local copies, waits for them, and re-layouts  3.34 us

profile of v2, /device:TPU:0, one launch (start us, length us, event | category | flops | bytes accessed | tf_op | source)
XLA Modules:
  0.0 54.4 jit_solution(8279762078482296867)
XLA Ops:
  0.6 50.5 %shard_map.104 = (f32[64,1024]{1,0:T(8,128)}, f32[64,1024]{1,0:T(8,128)}) custom-call(s32[1,3]{1,0:T(1,128)} %near_list.1, s32[1,2]{1,0:T(1,128)} %inverse_list.1, s32[3,1,4]{2,1,0:T(1,128)} %bitcast.1, bf16[64,1024]{1,0:T(8,128)(2,1)} %sides_hbm.1, bf16[1,3,1024,1024]{3,2,1,0:T(8,128)(2,1)} %near_hbm.1, bf16[1,2,1024,1024]{3,2,1,0:T(8,128)(2,1)} %inverse_hbm.1, ...), custom_call_target="tpu_custom_call" | custom-call | tf_op jit(solution)/shard_map/pallas_call | solution.py:403
  51.1 1.7 %copy.13 = f32[64,1024]{1,0:T(8,128)} copy(f32[64,1024]{1,0:T(8,128)} %get-tuple-element.4) | data formatting | bytes 524288
  52.8 1.7 %copy.14 = f32[64,1024]{1,0:T(8,128)} copy(f32[64,1024]{1,0:T(8,128)} %get-tuple-element.5) | data formatting | bytes 524288

commit v3 on v2

--- a/solution.py
+++ b/solution.py
@@ -314,19 +314,21 @@
 
     def operate(e, a):
         far_begin(a, e)
-        for c in range(CHUNKS - 1):
+        for c in range(CHUNKS // 2):
             relay(e, c)
         far_mid(a)
-        relay(e, CHUNKS - 1)
+        for c in range(CHUNKS // 2, CHUNKS):
+            relay(e, c)
         for c in range(CHUNKS - 1):
             pass_on(e, c)
             if c + 1 == CHUNKS // 2:
                 far_late(a)
-        for c in range(CHUNKS - 1):
+        for c in range(CHUNKS // 2):
             slots(e, c, near_at, near, "near")
         pass_on(e, CHUNKS - 1)
         fields = far_couple(a)
-        slots(e, CHUNKS - 1, near_at, near, "near")
+        for c in range(CHUNKS // 2, CHUNKS):
+            slots(e, c, near_at, near, "near")
         return own(e).astype(F32) + acc[...] + far_end(a, fields)
 
     for c in range(CHUNKS):

time: 54.6 us -> 52.5 us (0.962)
  Pallas kernels: 50.5 us -> 48.3 us
    pallas_call x1, Pallas kernels: 50.5 us -> 48.3 us  [shards(): pl.pallas_call(functools.partial(kernel, count), out_shape=(out, out), in...]
where the time goes in v3:
time: 52.5 us; the launch traced here: 52.3 us
  Pallas kernels  48.3 us (92%)
  local copies, waits for them, and re-layouts  3.34 us (6%)
  between operations  0.64 us (1%)
    pallas_call x1, Pallas kernels, shards(): pl.pallas_call(functools.partial(kernel, count), out_shape=(out, out), in...  48.3 us
    unnamed x2, local copies, waits for them, and re-layouts  3.34 us

profile of v3, /device:TPU:0, one launch (start us, length us, event | category | flops | bytes accessed | tf_op | source)
XLA Modules:
  0.0 52.3 jit_solution(4792582432092078429)
XLA Ops:
  0.6 48.3 %shard_map.104 = (f32[64,1024]{1,0:T(8,128)}, f32[64,1024]{1,0:T(8,128)}) custom-call(s32[1,3]{1,0:T(1,128)} %near_list.1, s32[1,2]{1,0:T(1,128)} %inverse_list.1, s32[3,1,4]{2,1,0:T(1,128)} %bitcast.1, bf16[64,1024]{1,0:T(8,128)(2,1)} %sides_hbm.1, bf16[1,3,1024,1024]{3,2,1,0:T(8,128)(2,1)} %near_hbm.1, bf16[1,2,1024,1024]{3,2,1,0:T(8,128)(2,1)} %inverse_hbm.1, ...), custom_call_target="tpu_custom_call" | custom-call | tf_op jit(solution)/shard_map/pallas_call | solution.py:405
  49.0 1.7 %copy.13 = f32[64,1024]{1,0:T(8,128)} copy(f32[64,1024]{1,0:T(8,128)} %get-tuple-element.4) | data formatting | bytes 524288
  50.6 1.7 %copy.14 = f32[64,1024]{1,0:T(8,128)} copy(f32[64,1024]{1,0:T(8,128)} %get-tuple-element.5) | data formatting | bytes 524288
